TPU v7x, 256 devices: a whole 4x4x8 slice. The times are simulated.
256 devices in a mesh: seq: 64 (over y, z, core), tp: 4 (over x).
Axes of the slice: x: 4, y: 4, z: 8, core: 2. Of those that a mesh axis runs over, the one named last changes fastest.
Arguments:
- stream: bfloat16 [8192, 2048], P('seq'), may hold values from -256 to 256
- lengths: int32 [6], replicated, may hold values from 1 to 7168, 8192 in all
- q_weight: bfloat16 [2048, 1536], P(None, 'tp'), may hold values from -0.125 to 0.125
- kv_down: bfloat16 [2048, 576], replicated, may hold values from -0.125 to 0.125
- latent_gain: float32 [512], replicated, may hold values from 0.1 to 1.9
- kv_up: bfloat16 [8, 512, 256], P('tp'), may hold values from -0.25 to 0.25
- out_weight: bfloat16 [1024, 2048], P('tp'), may hold values from -0.1875 to 0.1875
- moe_gain: float32 [2048], replicated, may hold values from 0.1 to 1.9
- routes: int32 [8192, 6], P('seq'), may hold values from 0 to 63, all different within a row; in each aligned block of 128 rows (0 to 127, 128 to 255, ...) at most 24 rows name the same one
- route_weight: float32 [8192, 6], P('seq'), may hold values from 0.05 to 0.5
- expert_gate: bfloat16 [64, 2048, 1408], P('seq', None, 'tp'), may hold values from -0.125 to 0.125
- expert_up: bfloat16 [64, 2048, 1408], P('seq', None, 'tp'), may hold values from -0.125 to 0.125
- expert_down: bfloat16 [64, 1408, 2048], P('seq', 'tp'), may hold values from -0.15625 to 0.15625
Outputs:
- layer_out: bfloat16 [8192, 2048], P('seq')
- latent_cache: bfloat16 [8192, 576], P('seq')
Inputs may be any that keep to these rules, and one draw needn't show every extreme that they name: 6 lengths summing to 8192, the longest exactly 7168. In each aligned block of 128 rows no expert is named by more than 24 routes, a bound that some block reaches.
All inputs are finite; a program needn't handle non-finite values.
Results may differ from a plain program's by a relative error of at most 0.0075.
Values may be sent and summed in bfloat16 or wider, within the bound.
A program may use at most 128 MiB of HBM per device.

v0:
```python
import jax
import jax.numpy as jnp
from jax import lax
from jax.sharding import PartitionSpec as P

D = 2048
NOPE = 128
ROPE = 64
LATENT = 512
VDIM = 128
THETA = 50000.0


def place(token_index, lengths):
    prompt_ends = jnp.cumsum(lengths)
    before = (prompt_ends[None, :] <= token_index[:, None]).astype(jnp.int32)
    segment = jnp.sum(before, axis=1)
    prompt_start = jnp.sum(before * lengths[None, :], axis=1)
    return (segment, token_index - prompt_start)


def angles(position):
    half_rope = ROPE // 2
    frequency = THETA ** (-2.0 * jnp.arange(half_rope, dtype=jnp.float32) / ROPE)
    angle_table = position.astype(jnp.float32)[:, None] * frequency[None, :]
    return (jnp.cos(angle_table), jnp.sin(angle_table))


def rotate(values, cos_table, sin_table):
    half_rope = ROPE // 2
    first_half = values[..., :half_rope]
    second = values[..., half_rope:]
    return jnp.concatenate(
        [first_half * cos_table - second * sin_table, first_half * sin_table + second * cos_table],
        axis=-1,
    )


def on_device(
    stream,
    lengths,
    q_weight,
    kv_down,
    latent_gain,
    kv_up,
    out_weight,
    moe_gain,
    routes,
    route_weight,
    expert_gate,
    expert_up,
    expert_down,
):
    tok_count = stream.shape[0]
    head_count = kv_up.shape[0]
    first_row = lax.axis_index("seq") * tok_count
    token_index = first_row + jnp.arange(tok_count, dtype=jnp.int32)
    segment, position = place(token_index, lengths)
    cos_table, sin_table = angles(position)
    kv_proj = jnp.dot(stream, kv_down, preferred_element_type=jnp.float32)
    compressed = kv_proj[:, :LATENT]
    factor = lax.rsqrt(jnp.mean(compressed * compressed, axis=1, keepdims=True) + 1e-06)
    latent = jnp.concatenate(
        [
            compressed * factor * latent_gain[None, :],
            rotate(kv_proj[:, LATENT:], cos_table, sin_table),
        ],
        axis=1,
    ).astype(jnp.bfloat16)
    tp_count = lax.axis_size("tp")
    tp_index = lax.axis_index("tp")
    kv_up_all = lax.all_gather(kv_up, "tp", axis=0, tiled=True)
    all_heads = kv_up_all.shape[0]
    q_proj = jnp.dot(stream, q_weight, preferred_element_type=jnp.float32).astype(jnp.bfloat16)
    q_proj = lax.all_gather(q_proj, "tp", axis=1, tiled=True)
    q_proj = q_proj.reshape(tok_count, all_heads, NOPE + ROPE)
    absorbed = jnp.einsum(
        "thj,hcj->thc",
        q_proj[:, :, :NOPE],
        kv_up_all[:, :, :NOPE],
        preferred_element_type=jnp.float32,
    )
    rotated = rotate(
        q_proj[:, :, NOPE:].astype(jnp.float32), cos_table[:, None, :], sin_table[:, None, :]
    )
    softmax_scale = (NOPE + ROPE) ** (-0.5)
    queries = (jnp.concatenate([absorbed, rotated], axis=2) * softmax_scale).astype(jnp.bfloat16)
    queries = queries.reshape(tok_count * all_heads, LATENT + ROPE)
    row_segment = jnp.repeat(segment, all_heads)
    row_index = jnp.repeat(token_index, all_heads)
    key_rows = tok_count // tp_count
    own_keys = lax.dynamic_slice_in_dim(latent, tp_index * key_rows, key_rows, 0)
    shard_rows = lax.all_gather(own_keys, "seq", axis=0, tiled=True)
    seq_count = shard_rows.shape[0] // key_rows
    key_index = (
        jnp.arange(seq_count, dtype=jnp.int32)[:, None] * tok_count
        + tp_index * key_rows
        + jnp.arange(key_rows, dtype=jnp.int32)[None, :]
    ).reshape(-1)
    key_segment, unused = place(key_index, lengths)
    allowed = (row_segment[:, None] == key_segment[None, :]) & (
        key_index[None, :] <= row_index[:, None]
    )
    scores = jnp.einsum("ra,ka->rk", queries, shard_rows, preferred_element_type=jnp.float32)
    block_peak = jnp.max(jnp.where(allowed, scores, -jnp.inf), axis=1)
    peak = jnp.maximum(jnp.full_like(block_peak, -1e30), block_peak)
    weights = jnp.where(allowed, jnp.exp(scores - peak[:, None]), 0.0)
    weight_sum = jnp.sum(weights, axis=1)
    context_sum = jnp.dot(
        weights.astype(jnp.bfloat16), shard_rows[:, :LATENT], preferred_element_type=jnp.float32
    ).reshape(tok_count, all_heads, LATENT)
    heads_part = jnp.einsum(
        "thc,hcv->thv",
        context_sum,
        kv_up_all[:, :, NOPE:].astype(jnp.float32),
        precision=lax.Precision.HIGHEST,
    )
    packed = jnp.concatenate(
        [
            heads_part,
            weight_sum.reshape(tok_count, all_heads, 1),
            peak.reshape(tok_count, all_heads, 1),
        ],
        axis=2,
    )
    packed = packed.reshape(tok_count, tp_count, head_count, VDIM + 2).transpose(1, 0, 2, 3)
    packed = lax.all_to_all(packed, "tp", split_axis=0, concat_axis=0, tiled=True)
    part_peak = packed[:, :, :, VDIM + 1]
    top_peak = jnp.max(part_peak, axis=0)
    rescale = jnp.exp(part_peak - top_peak[None])
    numerator = jnp.sum(packed[:, :, :, :VDIM] * rescale[..., None], axis=0)
    denominator = jnp.sum(packed[:, :, :, VDIM] * rescale, axis=0)
    heads_out = numerator / denominator[..., None]
    heads_out = heads_out.astype(jnp.bfloat16).reshape(tok_count, head_count * VDIM)
    partial_attention = jnp.dot(heads_out, out_weight, preferred_element_type=jnp.float32)
    tp_count = lax.axis_size("tp")
    col_width = D // tp_count
    col_start = lax.axis_index("tp") * col_width
    attention_part = lax.psum_scatter(
        partial_attention.astype(jnp.bfloat16), "tp", scatter_dimension=1, tiled=True
    ).astype(jnp.float32)
    stream_part = lax.dynamic_slice_in_dim(stream, col_start, col_width, 1)
    hidden = stream_part.astype(jnp.float32) + attention_part
    square_sum = lax.psum(jnp.sum(hidden * hidden, axis=1, keepdims=True), "tp")
    gain_part = lax.dynamic_slice_in_dim(moe_gain, col_start, col_width, 0)
    normed = (hidden * lax.rsqrt(square_sum / D + 1e-06) * gain_part[None, :]).astype(jnp.bfloat16)
    experts = lax.axis_size("seq")
    top_k = routes.shape[1]
    capacity = min(tok_count, max(2, 2 * tok_count * top_k // experts))
    flat_routes = routes.reshape(-1)
    onehot = (flat_routes[:, None] == jnp.arange(experts, dtype=jnp.int32)[None, :]).astype(
        jnp.int32
    )
    slot_rank = jnp.sum((jnp.cumsum(onehot, axis=0) - onehot) * onehot, axis=1)
    slot_index = flat_routes * capacity + slot_rank
    slot_table = (
        slot_index[:, None] == jnp.arange(experts * capacity, dtype=jnp.int32)[None, :]
    ).astype(jnp.bfloat16)
    placing = jnp.sum(slot_table.reshape(tok_count, top_k, experts * capacity), axis=1)
    outgoing = jnp.einsum("ts,td->sd", placing, normed, preferred_element_type=jnp.float32).astype(
        jnp.bfloat16
    )
    outgoing = outgoing.reshape(experts, capacity, col_width)
    chunk_count = 2
    chunk_slots = capacity // chunk_count
    returned_chunks = []
    for chunk in range(chunk_count):
        sending = outgoing[:, chunk * chunk_slots : (chunk + 1) * chunk_slots]
        received = lax.all_to_all(sending, "seq", split_axis=0, concat_axis=0, tiled=True)
        sources, slot_count, _ = received.shape
        flat_part = received.reshape(sources * slot_count, col_width)
        flat_rows = lax.all_gather(flat_part, "tp", axis=1, tiled=True)
        gate_act = jnp.dot(flat_rows, expert_gate[0], preferred_element_type=jnp.float32)
        up_act = jnp.dot(flat_rows, expert_up[0], preferred_element_type=jnp.float32)
        hidden_units = (jax.nn.silu(gate_act) * up_act).astype(jnp.bfloat16)
        expert_out = jnp.dot(
            hidden_units, expert_down[0], preferred_element_type=jnp.float32
        ).astype(jnp.bfloat16)
        expert_sum = lax.psum_scatter(expert_out, "tp", scatter_dimension=1, tiled=True)
        expert_sum = expert_sum.reshape(sources, slot_count, col_width)
        returned_chunks.append(
            lax.all_to_all(expert_sum, "seq", split_axis=0, concat_axis=0, tiled=True)
        )
    returned = jnp.concatenate(returned_chunks, axis=1)
    gathered = returned.reshape(experts * capacity, col_width)[slot_index].reshape(
        tok_count, top_k, col_width
    )
    moe = jnp.zeros((tok_count, col_width), jnp.float32)
    for route_slot in range(top_k):
        moe = moe + route_weight[:, route_slot][:, None] * gathered[:, route_slot].astype(
            jnp.float32
        )
    layer_part = (hidden + moe).astype(jnp.bfloat16)
    layer_out = lax.all_gather(layer_part, "tp", axis=1, tiled=True)
    return (layer_out, latent)


def solution(mesh):
    return jax.shard_map(
        on_device,
        mesh=mesh,
        in_specs=(
            P("seq", None),
            P(),
            P(None, "tp"),
            P(),
            P(),
            P("tp", None, None),
            P("tp", None),
            P(),
            P("seq", None),
            P("seq", None),
            P("seq", None, "tp"),
            P("seq", None, "tp"),
            P("seq", "tp", None),
        ),
        out_specs=(P("seq", None), P("seq", None)),
        check_vma=False,
    )
```

profile of v0, /device:TPU:32, one launch (start us, length us, event | category | flops | bytes accessed | tf_op | source)
XLA Modules:
  0.0 472.8 jit_solution(8885224359928597981)
XLA Ops:
  14.7 13.1 %all_gather.18 = bf16[128,1536]{1,0:T(8,128)(2,1)S(1)} all-gather(bf16[128,384]{1,0:T(8,128)(2,1)S(1)} %convolution_convert_fusion.4), channel_id=1, replica_groups=mesh['seq'=64,'tp'=4] {'tp'}, dimensions={1}, use_global_device_ids=true | all-gather | bytes 491520 | tf_op jit(solution)/shard_map/all_gather | solution.py:75
  30.7 15.1 %all-gather.5.cloned.1.call-done = bf16[8,512,256]{2,1,0:T(8,128)(2,1)} async-done(((bf16[2,512,256]{2,1,0:T(8,128)(2,1)}), bf16[8,512,256]{2,1,0:T(8,128)(2,1)}) %all-gather.5.cloned.1.call-update) | async-done | bytes 2097168 | tf_op jit(solution)/shard_map/all_gather | solution.py:72
  47.5 2.5 copy.143
  50.0 75.5 %all-gather.7.cloned.1.call-done = bf16[2048,576]{1,0:T(8,128)(2,1)} async-done(((bf16[32,576]{1,0:T(8,128)(2,1)}), bf16[2048,576]{1,0:T(8,128)(2,1)}) %all-gather.7.cloned.1.call-update) | async-done | bytes 2359312 | tf_op jit(solution)/shard_map/all_gather | solution.py:93
  125.5 8.6 %select_reduce_fusion = (f32[1024]{0:T(1024)S(1)}, f32[1024,2048]{1,0:T(8,128)}) fusion(s32[2048]{0:T(1024)S(1)} %add.144, s32[2048]{0:T(1024)S(1)} %convert_reduce_fusion, s32[1024]{0:T(1024)S(1)} %le.48, s32[1024]{0:T(1024)S(1)} %eq.54, bf16[2048,576]{1,0:T(8,128)(2,1)} %all-gather.7.cloned.1.call-done, f32[1024,32]{1,0:T(8,128)} %bitcast.153, ...), kind=kOutput, calls=%fused_computation.2 | convolution fusion | flops 2428763136 | bytes 13135872 | tf_op jit(solution)/shard_map/ra,ka->rk/dot_general | solution.py:104
  134.4 5.5 %fusion = f32[1024]{0:T(1024)S(1)} fusion(f32[1024,2048]{1,0:T(8,128)} %get-tuple-element.29, f32[1024]{0:T(1024)S(1)} %broadcast_maximum_fusion, s32[2048]{0:T(1024)S(1)} %add.144, s32[2048]{0:T(1024)S(1)} %convert_reduce_fusion, s32[1024]{0:T(1024)S(1)} %le.48, s32[1024]{0:T(1024)S(1)} %eq.54), kind=kLoop, calls=%fused_computation.4 | loop fusion | flops 12581888 | bytes 8421376 | tf_op jit(solution)/shard_map/reduce_sum | solution.py:108
  140.2 4.3 fusion.10
  148.2 14.0 %all_to_all.25 = f32[4,128,2,130]{1,2,3,0:T(2,128)S(1)} all-to-all(f32[4,128,2,130]{1,2,3,0:T(2,128)S(1)} %maximum_bitcast_fusion), channel_id=1, replica_groups=mesh['seq'=64,'tp'=4] {'tp'}, dimensions={0} | all-to-all | bytes 1064960 | tf_op jit(solution)/shard_map/all_to_all | solution.py:127
  168.3 16.3 %reduce-scatter.4.cloned.1.call-done = bf16[128,512]{1,0:T(8,128)(2,1)} async-done(((bf16[128,2048]{1,0:T(8,128)(2,1)}), bf16[128,512]{1,0:T(8,128)(2,1)}) %reduce-scatter.4.cloned.1.call-update) | async-done | bytes 131088 | tf_op jit(solution)/shard_map/reduce_scatter | solution.py:139
  185.7 8.4 %psum.7 = f32[128,1]{0,1:T(1,128)S(1)} all-reduce(f32[128,1]{0,1:T(1,128)S(1)} %bitcast.158), channel_id=1, replica_groups=mesh['seq'=64,'tp'=4] {'tp'}, use_global_device_ids=true, to_apply=%region_16.17 | all-reduce | flops 128 | bytes 1024 | tf_op jit(solution)/shard_map/psum | solution.py:144
  196.0 38.2 %all_to_all.26 = bf16[64,12,512]{2,1,0:T(8,128)(2,1)S(1)} all-to-all(bf16[64,12,512]{2,1,0:T(8,128)(2,1)S(1)} %get-tuple-element.4), channel_id=1, replica_groups=mesh['seq'=64,'tp'=4] {'seq'}, dimensions={0} | all-to-all | bytes 1572864 | tf_op jit(solution)/shard_map/all_to_all | solution.py:169
  235.3 34.5 %all_to_all.27 = bf16[64,12,512]{2,1,0:T(8,128)(2,1)S(1)} all-to-all(bf16[64,12,512]{2,1,0:T(8,128)(2,1)S(1)} %get-tuple-element.5), channel_id=1, replica_groups=mesh['seq'=64,'tp'=4] {'seq'}, dimensions={0} | all-to-all | bytes 1572864 | tf_op jit(solution)/shard_map/all_to_all | solution.py:169
  273.5 3.6 fusion.23
  277.2 7.8 %convolution_convert_fusion.1 = bf16[768,2048]{1,0:T(8,128)(2,1)} fusion(bf16[1,352,2048]{2,1,0:T(8,128)(2,1)S(1)} %copy-done.15, bf16[768,2048]{1,0:T(8,128)(2,1)} %all-gather.9.cloned.1.call-done, bf16[1,2048,352]{1,2,0:T(8,128)(2,1)} %param.24, f32[768,352]{0,1:T(8,128)S(1)} %fusion.23), kind=kOutput, calls=%fused_computation.10 | convolution fusion | flops 2217787392 | bytes 10256384 | tf_op jit(solution)/shard_map/dot_general | solution.py:176
  285.3 32.2 %all-gather.11.cloned.1.call-done = bf16[768,2048]{1,0:T(8,128)(2,1)} async-done(((bf16[768,512]{1,0:T(8,128)(2,1)}), bf16[768,2048]{1,0:T(8,128)(2,1)}) %all-gather.11.cloned.1.call-update) | async-done | bytes 3145744 | tf_op jit(solution)/shard_map/all_gather | solution.py:172
  317.4 3.2 fusion.21
  320.6 8.2 %convolution_convert_fusion = bf16[768,2048]{1,0:T(8,128)(2,1)} fusion(bf16[1,352,2048]{2,1,0:T(8,128)(2,1)} %param.25, bf16[768,2048]{1,0:T(8,128)(2,1)} %all-gather.11.cloned.1.call-done, bf16[1,2048,352]{1,2,0:T(8,128)(2,1)} %param.24, f32[768,352]{0,1:T(8,128)S(1)} %fusion.21), kind=kOutput, calls=%fused_computation.9 | convolution fusion | flops 2217787392 | bytes 10256384 | tf_op jit(solution)/shard_map/dot_general | solution.py:176
  328.9 32.0 %reduce-scatter.6.cloned.1.call-done = bf16[768,512]{1,0:T(8,128)(2,1)} async-done(((bf16[768,2048]{1,0:T(8,128)(2,1)}), bf16[768,512]{1,0:T(8,128)(2,1)}) %reduce-scatter.6.cloned.1.call-update) | async-done | bytes 786448 | tf_op jit(solution)/shard_map/reduce_scatter | solution.py:179
  363.1 10.5 %all-to-all-start.2 = ((bf16[64,12,512]{2,1,0:T(8,128)(2,1)}), bf16[64,12,512]{2,1,0:T(8,128)(2,1)S(1)}, u32[]{:S(2)}, u32[]{:S(2)}) async-start(bf16[64,12,512]{2,1,0:T(8,128)(2,1)} %reshape.278), calls=%async_computation.4 | async-start | bytes 2097152 | tf_op jit(solution)/shard_map/all_to_all | solution.py:182
  373.6 30.5 %reduce-scatter.8.cloned.1.call-done = bf16[768,512]{1,0:T(8,128)(2,1)} async-done(((bf16[768,2048]{1,0:T(8,128)(2,1)}), bf16[768,512]{1,0:T(8,128)(2,1)}) %reduce-scatter.8.cloned.1.call-update) | async-done | bytes 786448 | tf_op jit(solution)/shard_map/reduce_scatter | solution.py:179
  406.2 10.7 %all-to-all-start.4 = ((bf16[64,12,512]{2,1,0:T(8,128)(2,1)}), bf16[64,12,512]{2,1,0:T(8,128)(2,1)}, u32[]{:S(2)}, u32[]{:S(2)}) async-start(bf16[64,12,512]{2,1,0:T(8,128)(2,1)} %reshape.280), calls=%async_computation.7 | async-start | bytes 2097152 | tf_op jit(solution)/shard_map/all_to_all | solution.py:182
  417.6 27.1 %all-to-all-done.4 = bf16[64,12,512]{2,1,0:T(8,128)(2,1)} async-done(((bf16[64,12,512]{2,1,0:T(8,128)(2,1)}), bf16[64,12,512]{2,1,0:T(8,128)(2,1)}, u32[]{:S(2)}, u32[]{:S(2)}) %all-to-all-start.4) | async-done | bytes 786464 | tf_op jit(solution)/shard_map/all_to_all | solution.py:182
  446.4 2.7 gather_fusion
  451.7 13.4 %all_gather.23 = bf16[128,2048]{1,0:T(8,128)(2,1)S(1)} all-gather(bf16[128,512]{1,0:T(8,128)(2,1)S(1)} %fusion.52), channel_id=1, replica_groups=mesh['seq'=64,'tp'=4] {'tp'}, dimensions={1}, use_global_device_ids=true | all-gather | bytes 655360 | tf_op jit(solution)/shard_map/all_gather | solution.py:194
  (120 shorter events, 40.5 us)
Async XLA Ops:
  7.2 2.4 copy-start
  7.2 4.5 copy-start.11
  7.2 38.6 %all-gather.5.cloned.1.call-start = ((), (), s32[]{:S(2)}) async-start(), calls=%async_computation.8 | async-start | bytes 2621440 | tf_op jit(solution)/shard_map/all_gather | solution.py:72
  7.9 117.6 %all-gather.7.cloned.1.call-start = ((), (), s32[]{:S(2)}) async-start(), calls=%async_computation.9 | async-start | bytes 2662400 | tf_op jit(solution)/shard_map/all_gather | solution.py:93
  9.6 3.3 copy-start.3
  12.8 171.8 %reduce-scatter.4.cloned.1.call-start = ((), (), s32[]{:S(2)}) async-start(), calls=%async_computation.10 | async-start | bytes 655360 | tf_op jit(solution)/shard_map/reduce_scatter | solution.py:139
  47.5 78.0 %copy-start.8 = (f32[128,8,32]{2,1,0:T(8,128)S(1)}, f32[128,8,32]{2,1,0:T(8,128)}, u32[]{:S(2)}) copy-start(f32[128,8,32]{2,1,0:T(8,128)} %copy.86) | copy-start | bytes 393220
  134.4 5.8 %copy-start.2 = (f32[1024,2048]{1,0:T(8,128)S(1)}, f32[1024,2048]{1,0:T(8,128)}, u32[]{:S(2)}) copy-start(f32[1024,2048]{1,0:T(8,128)} %get-tuple-element.29) | copy-start | bytes 25165828
  140.2 4.3 copy-start.4
  147.3 15.2 %copy-start.6 = (bf16[256,2048]{1,0:T(8,128)(2,1)S(1)}, bf16[256,2048]{1,0:T(8,128)(2,1)}, u32[]{:S(2)}) copy-start(bf16[256,2048]{1,0:T(8,128)(2,1)} %param.19) | copy-start | bytes 3145732
  148.2 15.6 %copy-start.9 = (s32[128,6]{0,1:T(8,128)S(1)}, s32[128,6]{0,1:T(8,128)}, u32[]{:S(2)}) copy-start(s32[128,6]{0,1:T(8,128)} %param.21) | copy-start | bytes 9220
  163.7 109.8 %all-gather.9.cloned.1.call-start = ((), (), s32[]{:S(2)}) async-start(), calls=%async_computation.11 | async-start | bytes 3932160 | tf_op jit(solution)/shard_map/all_gather | solution.py:172
  235.3 82.1 %all-gather.11.cloned.1.call-start = ((), (), s32[]{:S(2)}) async-start(), calls=%async_computation.13 | async-start | bytes 3932160 | tf_op jit(solution)/shard_map/all_gather | solution.py:172
  271.0 6.2 %copy-start.15 = (bf16[1,352,2048]{2,1,0:T(8,128)(2,1)S(1)}, bf16[1,352,2048]{2,1,0:T(8,128)(2,1)}, u32[]{:S(2)}) copy-start(bf16[1,352,2048]{2,1,0:T(8,128)(2,1)} %param.25) | copy-start | bytes 4325380
  271.0 89.9 %reduce-scatter.6.cloned.1.call-start = ((), (), s32[]{:S(2)}) async-start(), calls=%async_computation.12 | async-start | bytes 3932160 | tf_op jit(solution)/shard_map/reduce_scatter | solution.py:179
  284.9 32.5 %copy-start.14 = (bf16[1,2048,352]{1,2,0:T(8,128)(2,1)S(1)}, bf16[1,2048,352]{1,2,0:T(8,128)(2,1)}, u32[]{:S(2)}) copy-start(bf16[1,2048,352]{1,2,0:T(8,128)(2,1)} %param.23) | copy-start | bytes 4325380
  284.9 119.1 %reduce-scatter.8.cloned.1.call-start = ((), (), s32[]{:S(2)}) async-start(), calls=%async_computation.14 | async-start | bytes 3932160 | tf_op jit(solution)/shard_map/reduce_scatter | solution.py:179
  363.1 43.1 %all-to-all-start.2 = ((bf16[64,12,512]{2,1,0:T(8,128)(2,1)}), bf16[64,12,512]{2,1,0:T(8,128)(2,1)S(1)}, u32[]{:S(2)}, u32[]{:S(2)}) async-start(bf16[64,12,512]{2,1,0:T(8,128)(2,1)} %reshape.278), calls=%async_computation.4 | async-start | bytes 2097152 | tf_op jit(solution)/shard_map/all_to_all | solution.py:182
  373.6 43.5 %copy-start.10 = (f32[128,6]{0,1:T(8,128)S(1)}, f32[128,6]{0,1:T(8,128)}, u32[]{:S(2)}) copy-start(f32[128,6]{0,1:T(8,128)} %param.22) | copy-start | bytes 9220
  406.2 38.5 %all-to-all-start.4 = ((bf16[64,12,512]{2,1,0:T(8,128)(2,1)}), bf16[64,12,512]{2,1,0:T(8,128)(2,1)}, u32[]{:S(2)}, u32[]{:S(2)}) async-start(bf16[64,12,512]{2,1,0:T(8,128)(2,1)} %reshape.280), calls=%async_computation.7 | async-start | bytes 2097152 | tf_op jit(solution)/shard_map/all_to_all | solution.py:182
  449.1 1.5 copy-start.5
  449.3 1.2 copy-start.12
  449.4 1.2 copy-start.13
  449.4 16.6 %copy-start.1 = (bf16[2048,576]{0,1:T(8,128)(2,1)S(1)}, bf16[2048,576]{0,1:T(8,128)(2,1)}, u32[]{:S(2)}) copy-start(bf16[2048,576]{0,1:T(8,128)(2,1)} %param.16) | copy-start | bytes 7077892
  (1 other events, 0.9 us)
Sparse Core Ops, SparseCore 0:
  9.8 35.8 all-gather.4
  48.5 76.9 all-gather.6
  163.8 20.7 reduce-scatter.3
  235.4 38.0 all-gather.8
  275.2 42.2 all-gather.10
  319.8 41.0 reduce-scatter.5
  363.5 40.5 reduce-scatter.7
where the time goes:
time: 474 us; the launch traced here: 473 us
  waiting for transfers between devices  232 us (49%)
  blocking collectives  122 us (26%)
  matrix products  46.1 us (10%)
  local copies, waits for them, and re-layouts  21.8 us (5%)
  starting transfers between devices  21.7 us (5%)
  other arithmetic  15.1 us (3%)
  between operations  14.7 us (3%)
    all_gather x1, waiting for transfers between devices, on_device(): shard_rows = lax.all_gather(own_keys, 'seq', axis=0, tiled=True)  75.5 us
    all_to_all x2, blocking collectives, on_device(): lax.all_to_all(sending, 'seq', split_axis=0, concat_axis=0, tiled=True)  72.7 us
    reduce_scatter x2, waiting for transfers between devices, on_device(): lax.psum_scatter(expert_out, 'tp', scatter_dimension=1, tiled=True)  62.5 us
    all_gather x2, waiting for transfers between devices, on_device(): flat_rows = lax.all_gather(flat_part, 'tp', axis=1, tiled=True)  34.6 us
    all_to_all x2, waiting for transfers between devices, on_device(): lax.all_to_all(expert_sum, 'seq', split_axis=0, concat_axis=0, tiled=True)  27.1 us
    all_to_all x2, starting transfers between devices, on_device(): lax.all_to_all(expert_sum, 'seq', split_axis=0, concat_axis=0, tiled=True)  21.2 us
    reduce_scatter x1, waiting for transfers between devices, on_device(): lax.psum_scatter(partial_attention.astype(jnp.bfloat16), 'tp', scatter_di...  16.3 us
    dot_general x2, matrix products, on_device(): jnp.dot(hidden_units, expert_down[0], preferred_element_type=jnp.float32)  16 us
  transfers between devices with their start and end apart: 9, of which 8 were waited for; matrix products, arithmetic and copies ran while one was open for 10% of the time, Pallas kernels for 0%

commit v1 on v0

--- a/solution.py
+++ b/solution.py
@@ -169,7 +169,12 @@
         received = lax.all_to_all(sending, "seq", split_axis=0, concat_axis=0, tiled=True)
         sources, slot_count, _ = received.shape
         flat_part = received.reshape(sources * slot_count, col_width)
-        flat_rows = lax.all_gather(flat_part, "tp", axis=1, tiled=True)
+        table = []
+        for _ in range(lax.axis_size("tp")):
+            table.append(flat_part)
+        moved = jnp.stack(table, 0)
+        carry_in = lax.all_to_all(moved, axis_name="tp", split_axis=0, concat_axis=0)
+        flat_rows = jnp.concatenate(carry_in, 1)
         gate_act = jnp.dot(flat_rows, expert_gate[0], preferred_element_type=jnp.float32)
         up_act = jnp.dot(flat_rows, expert_up[0], preferred_element_type=jnp.float32)
         hidden_units = (jax.nn.silu(gate_act) * up_act).astype(jnp.bfloat16)

time: 474 us -> 487 us (1.027)
  blocking collectives: 122 us -> 205 us
  waiting for transfers between devices: 232 us -> 162 us
    all_to_all x0 -> x2, blocking collectives: none -> 83.1 us  [on_device(): lax.all_to_all(moved, axis_name='tp', split_axis=0, concat_axis=0)]
    reduce_scatter x2, waiting for transfers between devices: 62.5 us -> 27.8 us  [on_device(): lax.psum_scatter(expert_out, 'tp', scatter_dimension=1, tiled=True)]
    all_gather x2 -> x0, waiting for transfers between devices: 34.6 us -> none  [on_device(): flat_rows = lax.all_gather(flat_part, 'tp', axis=1, tiled=True)]
  transfers between devices with their start and end apart: 9 -> 7, of which waited for: 8 -> 5; matrix products, arithmetic and copies ran while one was open for 10% -> 7% of each run, Pallas kernels for 0% -> 0%
where the time goes in v1:
time: 487 us; the launch traced here: 483 us
  blocking collectives  205 us (42%)
  waiting for transfers between devices  162 us (33%)
  matrix products  47.6 us (10%)
  local copies, waits for them, and re-layouts  20.9 us (4%)
  starting transfers between devices  17.7 us (4%)
  other arithmetic  15.4 us (3%)
  between operations  14.5 us (3%)
    all_to_all x2, blocking collectives, on_device(): lax.all_to_all(moved, axis_name='tp', split_axis=0, concat_axis=0)  83.1 us
    all_gather x1, waiting for transfers between devices, on_device(): shard_rows = lax.all_gather(own_keys, 'seq', axis=0, tiled=True)  75.5 us
    all_to_all x2, blocking collectives, on_device(): lax.all_to_all(sending, 'seq', split_axis=0, concat_axis=0, tiled=True)  72.6 us
    reduce_scatter x2, waiting for transfers between devices, on_device(): lax.psum_scatter(expert_out, 'tp', scatter_dimension=1, tiled=True)  27.8 us
    all_to_all x2, waiting for transfers between devices, on_device(): lax.all_to_all(expert_sum, 'seq', split_axis=0, concat_axis=0, tiled=True)  27.1 us
    all_to_all x2, starting transfers between devices, on_device(): lax.all_to_all(expert_sum, 'seq', split_axis=0, concat_axis=0, tiled=True)  17.5 us
    dot_general x2, matrix products, on_device(): jnp.dot(hidden_units, expert_down[0], preferred_element_type=jnp.float32)  16.7 us
    reduce_scatter x1, waiting for transfers between devices, on_device(): lax.psum_scatter(partial_attention.astype(jnp.bfloat16), 'tp', scatter_di...  16 us
  transfers between devices with their start and end apart: 7, of which 5 were waited for; matrix products, arithmetic and copies ran while one was open for 7% of the time, Pallas kernels for 0%

profile of v1, /device:TPU:32, one launch (start us, length us, event | category | flops | bytes accessed | tf_op | source)
XLA Modules:
  0.0 482.8 jit_solution(4789653768706131129)
XLA Ops:
  14.7 13.0 %all_gather.12 = bf16[128,1536]{1,0:T(8,128)(2,1)S(1)} all-gather(bf16[128,384]{1,0:T(8,128)(2,1)S(1)} %convolution_convert_fusion.4), channel_id=1, replica_groups=mesh['seq'=64,'tp'=4] {'tp'}, dimensions={1}, use_global_device_ids=true | all-gather | bytes 491520 | tf_op jit(solution)/shard_map/all_gather | solution.py:75
  30.7 15.1 %all-gather.3.cloned.1.call-done = bf16[8,512,256]{2,1,0:T(8,128)(2,1)} async-done(((bf16[2,512,256]{2,1,0:T(8,128)(2,1)}), bf16[8,512,256]{2,1,0:T(8,128)(2,1)}) %all-gather.3.cloned.1.call-update) | async-done | bytes 2097168 | tf_op jit(solution)/shard_map/all_gather | solution.py:72
  47.5 2.5 copy.151
  50.0 75.5 %all-gather.5.cloned.1.call-done = bf16[2048,576]{1,0:T(8,128)(2,1)} async-done(((bf16[32,576]{1,0:T(8,128)(2,1)}), bf16[2048,576]{1,0:T(8,128)(2,1)}) %all-gather.5.cloned.1.call-update) | async-done | bytes 2359312 | tf_op jit(solution)/shard_map/all_gather | solution.py:93
  125.5 8.8 %select_reduce_fusion = (f32[1024]{0:T(1024)S(1)}, f32[1024,2048]{1,0:T(8,128)}) fusion(s32[2048]{0:T(1024)S(1)} %add.144, s32[2048]{0:T(1024)S(1)} %convert_reduce_fusion, s32[1024]{0:T(1024)S(1)} %le.48, s32[1024]{0:T(1024)S(1)} %eq.54, bf16[2048,576]{1,0:T(8,128)(2,1)} %all-gather.5.cloned.1.call-done, f32[1024,32]{1,0:T(8,128)} %bitcast.159, ...), kind=kOutput, calls=%fused_computation.2 | convolution fusion | flops 2428763136 | bytes 13135872 | tf_op jit(solution)/shard_map/ra,ka->rk/dot_general | solution.py:104
  134.6 5.5 %fusion = f32[1024]{0:T(1024)S(1)} fusion(f32[1024,2048]{1,0:T(8,128)} %get-tuple-element.29, f32[1024]{0:T(1024)S(1)} %broadcast_maximum_fusion, s32[2048]{0:T(1024)S(1)} %add.144, s32[2048]{0:T(1024)S(1)} %convert_reduce_fusion, s32[1024]{0:T(1024)S(1)} %le.48, s32[1024]{0:T(1024)S(1)} %eq.54), kind=kLoop, calls=%fused_computation.4 | loop fusion | flops 12581888 | bytes 8421376 | tf_op jit(solution)/shard_map/reduce_sum | solution.py:108
  140.5 4.3 fusion.10
  148.4 14.0 %all_to_all.35 = f32[4,128,2,130]{1,2,3,0:T(2,128)S(1)} all-to-all(f32[4,128,2,130]{1,2,3,0:T(2,128)S(1)} %maximum_bitcast_fusion), channel_id=1, replica_groups=mesh['seq'=64,'tp'=4] {'tp'}, dimensions={0} | all-to-all | bytes 1064960 | tf_op jit(solution)/shard_map/all_to_all | solution.py:127
  168.9 16.0 %reduce-scatter.4.cloned.1.call-done = bf16[128,512]{1,0:T(8,128)(2,1)} async-done(((bf16[128,2048]{1,0:T(8,128)(2,1)}), bf16[128,512]{1,0:T(8,128)(2,1)}) %reduce-scatter.4.cloned.1.call-update) | async-done | bytes 131088 | tf_op jit(solution)/shard_map/reduce_scatter | solution.py:139
  185.9 8.3 %psum.7 = f32[128,1]{0,1:T(1,128)S(1)} all-reduce(f32[128,1]{0,1:T(1,128)S(1)} %bitcast.164), channel_id=1, replica_groups=mesh['seq'=64,'tp'=4] {'tp'}, use_global_device_ids=true, to_apply=%region_16.17 | all-reduce | flops 128 | bytes 1024 | tf_op jit(solution)/shard_map/psum | solution.py:144
  196.3 38.2 %all_to_all.36 = bf16[64,12,512]{2,1,0:T(8,128)(2,1)S(1)} all-to-all(bf16[64,12,512]{2,1,0:T(8,128)(2,1)S(1)} %get-tuple-element.4), channel_id=1, replica_groups=mesh['seq'=64,'tp'=4] {'seq'}, dimensions={0} | all-to-all | bytes 1572864 | tf_op jit(solution)/shard_map/all_to_all | solution.py:169
  235.1 41.5 %all_to_all.37 = bf16[4,768,512]{1,2,0:T(8,128)(2,1)} all-to-all(bf16[4,768,512]{1,2,0:T(8,128)(2,1)S(1)} %stack.6), channel_id=1, replica_groups=mesh['seq'=64,'tp'=4] {'tp'}, dimensions={0} | all-to-all | bytes 6291456 | tf_op jit(solution)/shard_map/all_to_all | solution.py:176
  276.6 4.2 fusion.21
  280.8 8.5 %convolution_convert_fusion.1 = bf16[768,2048]{1,0:T(8,128)(2,1)} fusion(bf16[1,352,2048]{2,1,0:T(8,128)(2,1)} %param.25, bf16[768,2048]{0,1:T(8,128)(2,1)} %bitcast.21, bf16[1,2048,352]{1,2,0:T(8,128)(2,1)} %param.24, f32[768,352]{0,1:T(8,128)} %fusion.21), kind=kOutput, calls=%fused_computation.10 | convolution fusion | flops 2217787392 | bytes 10256384 | tf_op jit(solution)/shard_map/dot_general | solution.py:181
  289.3 34.5 %all_to_all.38 = bf16[64,12,512]{2,1,0:T(8,128)(2,1)S(1)} all-to-all(bf16[64,12,512]{2,1,0:T(8,128)(2,1)S(1)} %get-tuple-element.5), channel_id=1, replica_groups=mesh['seq'=64,'tp'=4] {'seq'}, dimensions={0} | all-to-all | bytes 1572864 | tf_op jit(solution)/shard_map/all_to_all | solution.py:169
  324.4 41.6 %all_to_all.39 = bf16[4,768,512]{1,2,0:T(8,128)(2,1)} all-to-all(bf16[4,768,512]{1,2,0:T(8,128)(2,1)S(1)} %stack.7), channel_id=1, replica_groups=mesh['seq'=64,'tp'=4] {'tp'}, dimensions={0} | all-to-all | bytes 6291456 | tf_op jit(solution)/shard_map/all_to_all | solution.py:176
  366.1 3.2 fusion.23
  369.2 8.2 %convolution_convert_fusion = bf16[768,2048]{1,0:T(8,128)(2,1)} fusion(bf16[1,352,2048]{2,1,0:T(8,128)(2,1)} %param.25, bf16[768,2048]{0,1:T(8,128)(2,1)} %bitcast.27, bf16[1,2048,352]{1,2,0:T(8,128)(2,1)} %param.24, f32[768,352]{0,1:T(8,128)S(1)} %fusion.23), kind=kOutput, calls=%fused_computation.9 | convolution fusion | flops 2217787392 | bytes 10256384 | tf_op jit(solution)/shard_map/dot_general | solution.py:181
  379.7 6.8 %all-to-all-start.3 = ((bf16[64,12,512]{2,1,0:T(8,128)(2,1)}), bf16[64,12,512]{2,1,0:T(8,128)(2,1)S(1)}, u32[]{:S(2)}, u32[]{:S(2)}) async-start(bf16[64,12,512]{2,1,0:T(8,128)(2,1)} %reshape.289), calls=%async_computation.5 | async-start | bytes 2097152 | tf_op jit(solution)/shard_map/all_to_all | solution.py:187
  386.5 27.7 %reduce-scatter.8.cloned.1.call-done = bf16[768,512]{1,0:T(8,128)(2,1)} async-done(((bf16[768,2048]{1,0:T(8,128)(2,1)}), bf16[768,512]{1,0:T(8,128)(2,1)}) %reduce-scatter.8.cloned.1.call-update) | async-done | bytes 786448 | tf_op jit(solution)/shard_map/reduce_scatter | solution.py:184
  416.3 10.7 %all-to-all-start.6 = ((bf16[64,12,512]{2,1,0:T(8,128)(2,1)}), bf16[64,12,512]{2,1,0:T(8,128)(2,1)}, u32[]{:S(2)}, u32[]{:S(2)}) async-start(bf16[64,12,512]{2,1,0:T(8,128)(2,1)} %reshape.292), calls=%async_computation.9 | async-start | bytes 2097152 | tf_op jit(solution)/shard_map/all_to_all | solution.py:187
  427.7 27.1 %all-to-all-done.6 = bf16[64,12,512]{2,1,0:T(8,128)(2,1)} async-done(((bf16[64,12,512]{2,1,0:T(8,128)(2,1)}), bf16[64,12,512]{2,1,0:T(8,128)(2,1)}, u32[]{:S(2)}, u32[]{:S(2)}) %all-to-all-start.6) | async-done | bytes 786464 | tf_op jit(solution)/shard_map/all_to_all | solution.py:187
  456.5 2.7 gather_fusion
  461.9 13.4 %all_gather.15 = bf16[128,2048]{1,0:T(8,128)(2,1)S(1)} all-gather(bf16[128,512]{1,0:T(8,128)(2,1)S(1)} %fusion.52), channel_id=1, replica_groups=mesh['seq'=64,'tp'=4] {'tp'}, dimensions={1}, use_global_device_ids=true | all-gather | bytes 655360 | tf_op jit(solution)/shard_map/all_gather | solution.py:199
  (120 shorter events, 37.1 us)
Async XLA Ops:
  7.2 2.4 copy-start
  7.2 4.6 copy-start.11
  7.2 38.6 %all-gather.3.cloned.1.call-start = ((), (), s32[]{:S(2)}) async-start(), calls=%async_computation.10 | async-start | bytes 2621440 | tf_op jit(solution)/shard_map/all_gather | solution.py:72
  7.9 117.6 %all-gather.5.cloned.1.call-start = ((), (), s32[]{:S(2)}) async-start(), calls=%async_computation.11 | async-start | bytes 2662400 | tf_op jit(solution)/shard_map/all_gather | solution.py:93
  9.6 3.3 copy-start.3
  11.9 0.9 copy-start.7
  12.8 172.1 %reduce-scatter.4.cloned.1.call-start = ((), (), s32[]{:S(2)}) async-start(), calls=%async_computation.12 | async-start | bytes 655360 | tf_op jit(solution)/shard_map/reduce_scatter | solution.py:139
  47.5 78.0 %copy-start.8 = (f32[128,8,32]{2,1,0:T(8,128)S(1)}, f32[128,8,32]{2,1,0:T(8,128)}, u32[]{:S(2)}) copy-start(f32[128,8,32]{2,1,0:T(8,128)} %copy.92) | copy-start | bytes 393220
  134.6 5.8 %copy-start.2 = (f32[1024,2048]{1,0:T(8,128)S(1)}, f32[1024,2048]{1,0:T(8,128)}, u32[]{:S(2)}) copy-start(f32[1024,2048]{1,0:T(8,128)} %get-tuple-element.29) | copy-start | bytes 25165828
  140.5 4.3 copy-start.4
  147.6 15.2 %copy-start.6 = (bf16[256,2048]{1,0:T(8,128)(2,1)S(1)}, bf16[256,2048]{1,0:T(8,128)(2,1)}, u32[]{:S(2)}) copy-start(bf16[256,2048]{1,0:T(8,128)(2,1)} %param.19) | copy-start | bytes 3145732
  148.4 15.6 %copy-start.9 = (s32[128,6]{0,1:T(8,128)S(1)}, s32[128,6]{0,1:T(8,128)}, u32[]{:S(2)}) copy-start(s32[128,6]{0,1:T(8,128)} %param.21) | copy-start | bytes 9220
  164.0 213.5 %reduce-scatter.6.cloned.1.call-start = ((), (), s32[]{:S(2)}) async-start(), calls=%async_computation.13 | async-start | bytes 3932160 | tf_op jit(solution)/shard_map/reduce_scatter | solution.py:184
  235.1 41.5 %copy-start.14 = (bf16[1,2048,352]{1,2,0:T(8,128)(2,1)S(1)}, bf16[1,2048,352]{1,2,0:T(8,128)(2,1)}, u32[]{:S(2)}) copy-start(bf16[1,2048,352]{1,2,0:T(8,128)(2,1)} %param.23) | copy-start | bytes 4325380
  289.2 125.0 %reduce-scatter.8.cloned.1.call-start = ((), (), s32[]{:S(2)}) async-start(), calls=%async_computation.14 | async-start | bytes 3932160 | tf_op jit(solution)/shard_map/reduce_scatter | solution.py:184
  324.4 41.7 %copy-start.15 = (bf16[1,2048,352]{1,2,0:T(8,128)(2,1)S(1)}, bf16[1,2048,352]{1,2,0:T(8,128)(2,1)}, u32[]{:S(2)}) copy-start(bf16[1,2048,352]{1,2,0:T(8,128)(2,1)} %param.23) | copy-start | bytes 4325380
  379.7 36.7 %all-to-all-start.3 = ((bf16[64,12,512]{2,1,0:T(8,128)(2,1)}), bf16[64,12,512]{2,1,0:T(8,128)(2,1)S(1)}, u32[]{:S(2)}, u32[]{:S(2)}) async-start(bf16[64,12,512]{2,1,0:T(8,128)(2,1)} %reshape.289), calls=%async_computation.5 | async-start | bytes 2097152 | tf_op jit(solution)/shard_map/all_to_all | solution.py:187
  386.5 40.7 %copy-start.10 = (f32[128,6]{0,1:T(8,128)S(1)}, f32[128,6]{0,1:T(8,128)}, u32[]{:S(2)}) copy-start(f32[128,6]{0,1:T(8,128)} %param.22) | copy-start | bytes 9220
  416.3 38.5 %all-to-all-start.6 = ((bf16[64,12,512]{2,1,0:T(8,128)(2,1)}), bf16[64,12,512]{2,1,0:T(8,128)(2,1)}, u32[]{:S(2)}, u32[]{:S(2)}) async-start(bf16[64,12,512]{2,1,0:T(8,128)(2,1)} %reshape.292), calls=%async_computation.9 | async-start | bytes 2097152 | tf_op jit(solution)/shard_map/all_to_all | solution.py:187
  459.2 1.5 copy-start.5
  459.5 1.2 copy-start.12
  459.5 1.2 copy-start.13
  459.5 16.6 %copy-start.1 = (bf16[2048,576]{0,1:T(8,128)(2,1)S(1)}, bf16[2048,576]{0,1:T(8,128)(2,1)}, u32[]{:S(2)}) copy-start(bf16[2048,576]{0,1:T(8,128)(2,1)} %param.16) | copy-start | bytes 7077892
Sparse Core Ops, SparseCore 0:
  9.8 35.8 all-gather.2
  48.5 76.9 all-gather.4
  164.1 20.7 reduce-scatter.3
  289.4 36.5 reduce-scatter.5
  377.6 36.5 reduce-scatter.7
